TPU v7x, 256 devices: a whole 4x4x8 slice. The times are simulated.
256 devices in a mesh: req: 8 (over z_lo, y), dev: 32 (over z_hi, x, core).
Axes of the slice: x: 4, y: 4, z: 8 (z_hi: 4, z_lo: 2; z = z_hi * 2 + z_lo), core: 2. Of those that a mesh axis runs over, the one named last changes fastest.
Arguments:
- hidden_in: bfloat16 [8, 1024, 2048], P('req', 'dev'), may hold values from -60 to 60
- attention_gain: float32 [2048], replicated, may hold values from 0.1 to 1.9
- query_weight: bfloat16 [2048, 2048], P('dev'), may hold values from -0.625 to 0.625
- keyval_weight: bfloat16 [1024, 2048], P('dev'), may hold values from -0.5 to 0.5
- out_weight: bfloat16 [2048, 2048], P('dev'), may hold values from -0.0625 to 0.0625
- feedforward_gain: float32 [2048], replicated, may hold values from 0.1 to 1.9
- gate_weight: bfloat16 [8192, 2048], P(('req', 'dev')), may hold values from -0.125 to 0.125
- up_weight: bfloat16 [8192, 2048], P(('req', 'dev')), may hold values from -0.125 to 0.125
- down_weight: bfloat16 [8192, 2048], P(('req', 'dev')), may hold values from -0.0625 to 0.0625
- prefix_pool: bfloat16 [8, 256, 16, 8, 128], P('req', 'dev'), may hold values from -640 to 640
- page_table: int32 [8, 256], P('req'), may hold values from 0 to 255, each once within a row
- prefix_length: int32 [8], P('req'), may hold values from 1 to 4096, 20480 in all
Outputs:
- hidden_out: bfloat16 [8, 1024, 2048], P('req', 'dev')
- new_keyval: bfloat16 [8, 1024, 8, 128], P('req', 'dev')
Inputs may be any that keep to these rules, and one draw needn't show every extreme that they name: `page_table`: each row names every page of the request's pool once. `prefix_length`: the longest cached prefix is exactly 4096.
All inputs are finite; a program needn't handle non-finite values. No bound on the sum of `prefix_length` on one device may be relied on, other than what follows from the above.
Results may differ from a plain program's by a relative error of at most 0.013.
The roundings to bfloat16 on the way count: a program that leaves them out, or rounds other values in their place, can miss the bound.
Values may be sent and summed in bfloat16 or wider, within the bound.
A program may use at most 64 MiB of HBM per device.

v0:
```python
import jax
import jax.numpy as jnp
from jax import lax
from jax.sharding import PartitionSpec as P

HQ = 32
KVH = 8
HD = 64
PAGE = 16
KBLOCK = 512
ROPE_BASE = 10000000.0
EPS = 1e-05
ATTENTION_SCALE = 0.015625
MASKED = -1e30


def root_norm(activations, norm_gain):
    widened = activations.astype(jnp.float32)
    inverse_rms = lax.rsqrt(jnp.mean(widened * widened, axis=-1, keepdims=True) + EPS)
    return (widened * inverse_rms * norm_gain).astype(jnp.bfloat16)


def rotate(vector, positions):
    half_width = vector.shape[-1] // 2
    frequency = ROPE_BASE ** (-jnp.arange(half_width, dtype=jnp.float32) / half_width)
    angles = positions.astype(jnp.float32)[:, None] * frequency[None, :]
    cosine = jnp.cos(angles)[:, None, :]
    sine_part = jnp.sin(angles)[:, None, :]
    leading = vector[..., :half_width]
    trailing = vector[..., half_width:]
    return jnp.concatenate(
        [leading * cosine - trailing * sine_part, trailing * cosine + leading * sine_part], axis=-1
    )


def transposed_product(left, right):
    return lax.dot_general(
        left, right, (((1,), (1,)), ((), ())), preferred_element_type=jnp.float32
    )


def attend_block(carried, queries, key_part, value_part, allowed):
    row_max, row_total, summed = carried
    scores = transposed_product(queries, key_part)
    scores = jnp.where(allowed, scores, MASKED)
    new_max = jnp.maximum(row_max, jnp.max(scores, axis=1))
    factor = jnp.exp(row_max - new_max)
    weights = jnp.where(allowed, jnp.exp(scores - new_max[:, None]), 0.0)
    new_total = row_total * factor + jnp.sum(weights, axis=1)
    summed = summed * factor[:, None] + jnp.dot(
        weights.astype(jnp.bfloat16), value_part, preferred_element_type=jnp.float32
    )
    return (new_max, new_total, summed)


def on_device(
    hidden_in,
    attention_gain,
    query_weight,
    keyval_weight,
    out_weight,
    feedforward_gain,
    gate_weight,
    up_weight,
    down_weight,
    prefix_pool,
    page_table,
    prefix_length,
):
    local_tokens = hidden_in.shape[1]
    device_count = lax.axis_size("dev")
    all_count = local_tokens * device_count
    heads_here = query_weight.shape[0] // HD
    group_size = HQ // KVH
    member = lax.axis_index("dev")
    length = prefix_length[0]
    own_tokens = hidden_in[0]
    all_tokens = lax.all_gather(own_tokens, "dev", axis=0, tiled=True)
    normed = root_norm(all_tokens, attention_gain)
    positions = length + jnp.arange(all_count, dtype=jnp.int32)
    raw_columns = transposed_product(keyval_weight, normed).astype(jnp.bfloat16)
    keyval_all = lax.all_gather(raw_columns, "dev", axis=0, tiled=True)
    own_rows = lax.dynamic_slice_in_dim(
        keyval_all, member * local_tokens, local_tokens, 1
    ).T.reshape(local_tokens, KVH, 2 * HD)
    own_positions = lax.dynamic_slice_in_dim(positions, member * local_tokens, local_tokens, 0)
    own_keys = rotate(own_rows[..., :HD].astype(jnp.float32), own_positions).astype(jnp.bfloat16)
    new_keyval = jnp.concatenate([own_keys, own_rows[..., HD:]], axis=-1)
    shared_head = member * heads_here // group_size
    head_pair = lax.dynamic_slice_in_dim(keyval_all, shared_head * 2 * HD, 2 * HD, 0).T
    fresh_keys = rotate(head_pair[:, None, :HD].astype(jnp.float32), positions)[:, 0, :].astype(
        jnp.bfloat16
    )
    fresh_values = head_pair[:, HD:]
    query_full = transposed_product(normed, query_weight).reshape(all_count, heads_here, HD)
    queries = (
        (rotate(query_full, positions) * ATTENTION_SCALE)
        .astype(jnp.bfloat16)
        .reshape(all_count * heads_here, HD)
    )
    local_pool = prefix_pool[0]
    wanted = jnp.arange(device_count, dtype=jnp.int32) * heads_here // group_size
    outgoing = jnp.take(local_pool, wanted, axis=2)
    incoming = lax.all_to_all(outgoing, "dev", split_axis=2, concat_axis=0, tiled=True)
    pool_head = incoming[:, :, 0, :]
    page_rows = page_table[0]
    block_pages = KBLOCK // PAGE
    query_rows = all_count * heads_here
    carried = (
        jnp.full((query_rows,), MASKED, jnp.float32),
        jnp.zeros((query_rows,), jnp.float32),
        jnp.zeros((query_rows, HD), jnp.float32),
    )

    def prefix_step(block_index, running):
        page_ids = lax.dynamic_slice_in_dim(page_rows, block_index * block_pages, block_pages, 0)
        stored = jnp.take(pool_head, page_ids, axis=0).reshape(KBLOCK, 2 * HD)
        slot_ids = block_index * KBLOCK + jnp.arange(KBLOCK, dtype=jnp.int32)
        allowed = (slot_ids < length)[None, :]
        return attend_block(running, queries, stored[:, :HD], stored[:, HD:], allowed)

    block_count = (length + KBLOCK - 1) // KBLOCK
    carried = lax.fori_loop(0, block_count, prefix_step, carried)
    query_token = jnp.arange(query_rows, dtype=jnp.int32) // heads_here
    causal = jnp.arange(all_count, dtype=jnp.int32)[None, :] <= query_token[:, None]
    row_max, row_total, summed = attend_block(carried, queries, fresh_keys, fresh_values, causal)
    attended = (summed / row_total[:, None]).astype(jnp.bfloat16)
    rows_in = attended
    attention_own = lax.psum_scatter(
        jnp.dot(rows_in, out_weight, preferred_element_type=jnp.float32).astype(jnp.bfloat16),
        "dev",
        scatter_dimension=0,
        tiled=True,
    ).astype(jnp.float32)
    residual = own_tokens.astype(jnp.float32) + attention_own
    mlp_rows = lax.all_gather(root_norm(residual, feedforward_gain), "dev", axis=0, tiled=True)
    fetched = (
        lax.all_gather(gate_weight, "req", axis=0, tiled=True),
        lax.all_gather(up_weight, "req", axis=0, tiled=True),
        lax.all_gather(down_weight, "req", axis=0, tiled=True),
    )
    gate_rows, up_rows, down_rows = fetched
    rows_in = mlp_rows
    gate_act = transposed_product(rows_in, gate_rows)
    up_act = transposed_product(rows_in, up_rows)
    activated = (jax.nn.silu(gate_act) * up_act).astype(jnp.bfloat16)
    feedforward_own = lax.psum_scatter(
        jnp.dot(activated, down_rows, preferred_element_type=jnp.float32).astype(jnp.bfloat16),
        "dev",
        scatter_dimension=0,
        tiled=True,
    ).astype(jnp.float32)
    hidden_out = (residual + feedforward_own).astype(jnp.bfloat16)
    return (hidden_out[None], new_keyval[None])


def solution(mesh):
    placed = (
        P("req", "dev", None),
        P(),
        P("dev", None),
        P("dev", None),
        P("dev", None),
        P(),
        P(("req", "dev"), None),
        P(("req", "dev"), None),
        P(("req", "dev"), None),
        P("req", "dev", None, None, None),
        P("req", None),
        P("req"),
    )
    return jax.shard_map(
        on_device,
        mesh=mesh,
        in_specs=placed,
        out_specs=(P("req", "dev", None), P("req", "dev", None, None)),
        check_vma=False,
    )
```

profile of v0, /device:TPU:8, one launch (start us, length us, event | category | flops | bytes accessed | tf_op | source)
XLA Modules:
  0.0 542.3 jit_solution(16338885161745345462)
XLA Ops:
  8.1 0.7 all-gather.18.cloned.1.call-update
  8.8 65.8 %all-gather.18.cloned.1.call-done = bf16[1,1024,2048]{2,1,0:T(8,128)(2,1)} async-done(((bf16[1,32,2048]{2,1,0:T(8,128)(2,1)}), bf16[1,1024,2048]{2,1,0:T(8,128)(2,1)}) %all-gather.18.cloned.1.call-update) | async-done | bytes 4194320 | tf_op jit(solution)/shard_map/all_gather | solution.py:78
  74.6 3.2 fusion.11
  78.1 2.1 fusion.34
  80.2 0.8 gather_fusion.1
  81.1 1.1 select_bitcast_fusion
  82.2 6.6 %all-to-all-start = ((bf16[8,16,32,128]{3,1,0,2:T(8,128)(2,1)}), bf16[8,16,32,128]{3,1,0,2:T(8,128)(2,1)S(1)}, u32[]{:S(2)}, u32[]{:S(2)}) async-start(bf16[8,16,32,128]{3,1,0,2:T(8,128)(2,1)} %select_bitcast_fusion), calls=%async_computation | async-start | bytes 2097152 | tf_op jit(solution)/shard_map/all_to_all | solution.py:104
  89.6 3.7 fusion.25
  93.3 55.0 %all-gather.8.cloned.1.call-done = bf16[1024,1024]{1,0:T(8,128)(2,1)} async-done(((bf16[32,1024]{1,0:T(8,128)(2,1)}), bf16[1024,1024]{1,0:T(8,128)(2,1)}) %all-gather.8.cloned.1.call-update) | async-done | bytes 2097168 | tf_op jit(solution)/shard_map/all_gather | solution.py:82
  148.3 1.0 dynamic-slice_bitcast_fusion
  150.2 13.3 %while.14 = (s32[]{:T(128)}, f32[1024]{0:T(1024)S(1)}, f32[1024]{0:T(1024)S(1)}, f32[1024,64]{0,1:T(8,128)S(1)}, s32[]{:T(128)}, /*index=5*/s32[]{:T(128)}, s32[...) while((s32[]{:T(128)}, f32[1024]{0:T(1024)S(1)}, ...), condition=%wide.region_4.5_spmd, body=%wide.region_1.4_spmd.sunk | while | flops 139661504 | bytes 7807763 | solution.py:123
  150.2 0.7 add_compare_fusion.2
  153.5 0.7 add_compare_fusion.2
  156.9 0.7 add_compare_fusion.2
  159.5 0.6 convolution_add_fusion.2
  160.2 0.7 add_compare_fusion.2
  163.5 0.8 fusion.15
  164.3 2.0 copy-done.1
  166.7 5.8 %convolution_convert_fusion.1 = bf16[1024,2048]{1,0:T(8,128)(2,1)} fusion(bf16[64,2048]{1,0:T(8,128)(2,1)S(1)} %copy-done, f32[1024,1024]{0,1:T(8,128)} %copy-done.1, f32[1024]{0:T(1024)S(1)} %max.6, f32[1024,64]{0,1:T(8,128)S(1)} %get-tuple-element.52, bf16[1024,128]{0,1:T(8,128)(2,1)S(1)} %dynamic-slice_bitcast_fusion, f32[1024]{0:T(1024)S(1)} %get-tuple-element.95, ...), kind=kOutput, calls=%fused_computation.31 | convolution fusion | flops 410255360 | bytes 9056256 | tf_op jit(solution)/shard_map/dot_general | solution.py:130
  173.2 108.5 %reduce-scatter.3.cloned.1.call-done = bf16[32,2048]{1,0:T(8,128)(2,1)} async-done(((bf16[1024,2048]{1,0:T(8,128)(2,1)}), bf16[32,2048]{1,0:T(8,128)(2,1)}) %reduce-scatter.3.cloned.1.call-update) | async-done | bytes 131088 | tf_op jit(solution)/shard_map/reduce_scatter | solution.py:129
  281.7 1.1 multiply_reduce_fusion
  282.8 1.7 multiply_convert_fusion
  285.1 0.7 all-gather.16.cloned.1.call-update
  286.0 56.1 %all-gather.10.cloned.1.call-done = bf16[1024,2048]{1,0:T(8,128)(2,1)} async-done(((bf16[32,2048]{1,0:T(8,128)(2,1)}), bf16[1024,2048]{1,0:T(8,128)(2,1)}) %all-gather.10.cloned.1.call-update) | async-done | bytes 4194320 | tf_op jit(solution)/shard_map/all_gather | solution.py:136
  342.1 3.8 fusion.87
  345.9 34.9 %all-gather.14.cloned.1.call-done = bf16[256,2048]{1,0:T(8,128)(2,1)} async-done(((bf16[32,2048]{1,0:T(8,128)(2,1)}), bf16[256,2048]{1,0:T(8,128)(2,1)}) %all-gather.14.cloned.1.call-update) | async-done | bytes 1048592 | tf_op jit(solution)/shard_map/all_gather | solution.py:139
  380.8 42.4 %all-gather.16.cloned.1.call-done = bf16[256,2048]{1,0:T(8,128)(2,1)} async-done(((bf16[32,2048]{1,0:T(8,128)(2,1)}), bf16[256,2048]{1,0:T(8,128)(2,1)}) %all-gather.16.cloned.1.call-update) | async-done | bytes 1048592 | tf_op jit(solution)/shard_map/all_gather | solution.py:140
  423.2 9.2 %convolution_convert_fusion = bf16[1024,2048]{1,0:T(8,128)(2,1)} fusion(bf16[256,2048]{1,0:T(8,128)(2,1)} %all-gather.16.cloned.1.call-done, bf16[1024,2048]{1,0:T(8,128)(2,1)} %all-gather.10.cloned.1.call-done, bf16[256,2048]{1,0:T(8,128)(2,1)} %all-gather.14.cloned.1.call-done, f32[1024,256]{1,0:T(8,128)S(1)} %fusion.87), kind=kOutput, calls=%fused_computation.30 | convolution fusion | flops 2151153664 | bytes 11534336 | tf_op jit(solution)/shard_map/dot_general | solution.py:148
  432.6 1.1 constant_dynamic-slice_fusion
  434.1 0.7 maximum_bitcast_fusion.2
  434.9 98.5 %reduce-scatter.5.cloned.1.call-done = bf16[32,2048]{1,0:T(8,128)(2,1)} async-done(((bf16[1024,2048]{1,0:T(8,128)(2,1)}), bf16[32,2048]{1,0:T(8,128)(2,1)}) %reduce-scatter.5.cloned.1.call-update) | async-done | bytes 131088 | tf_op jit(solution)/shard_map/reduce_scatter | solution.py:147
  533.4 1.6 fusion.69
  (110 shorter events, 13.6 us)
Async XLA Ops:
  8.0 158.7 %copy-start = (bf16[64,2048]{1,0:T(8,128)(2,1)S(1)}, bf16[64,2048]{1,0:T(8,128)(2,1)}, u32[]{:S(2)}) copy-start(bf16[64,2048]{1,0:T(8,128)(2,1)} %param.18) | copy-start | bytes 786436
  8.0 69.8 %copy-start.10 = (f32[2048]{0:T(1024)S(1)}, f32[2048]{0:T(1024)}, u32[]{:S(2)}) copy-start(f32[2048]{0:T(1024)} %param.15) | copy-start | bytes 24580
  8.0 69.8 %copy-start.9 = (bf16[32,2048]{1,0:T(8,128)(2,1)S(1)}, bf16[32,2048]{1,0:T(8,128)(2,1)}, u32[]{:S(2)}) copy-start(bf16[32,2048]{1,0:T(8,128)(2,1)} %param.17) | copy-start | bytes 393220
  8.0 66.6 %all-gather.18.cloned.1.call-start = ((), (), s32[]{:S(2)}) async-start(), calls=%async_computation.10 | async-start | bytes 4325376 | tf_op jit(solution)/shard_map/all_gather | solution.py:78
  8.8 139.5 %all-gather.8.cloned.1.call-start = ((), (), s32[]{:S(2)}) async-start(), calls=%async_computation.3 | async-start | bytes 2162688 | tf_op jit(solution)/shard_map/all_gather | solution.py:82
  74.6 3.4 copy-start.2
  78.1 2.1 copy-start.5
  80.1 9.5 %copy-start.8 = (bf16[64,2048]{1,0:T(8,128)(2,1)S(1)}, bf16[64,2048]{1,0:T(8,128)(2,1)}, u32[]{:S(2)}) copy-start(bf16[64,2048]{1,0:T(8,128)(2,1)} %param.16) | copy-start | bytes 786436
  82.2 67.9 %all-to-all-start = ((bf16[8,16,32,128]{3,1,0,2:T(8,128)(2,1)}), bf16[8,16,32,128]{3,1,0,2:T(8,128)(2,1)S(1)}, u32[]{:S(2)}, u32[]{:S(2)}) async-start(bf16[8,16,32,128]{3,1,0,2:T(8,128)(2,1)} %select_bitcast_fusion), calls=%async_computation | async-start | bytes 2097152 | tf_op jit(solution)/shard_map/all_to_all | solution.py:104
  88.8 192.9 %reduce-scatter.3.cloned.1.call-start = ((), (), s32[]{:S(2)}) async-start(), calls=%async_computation.4 | async-start | bytes 4325376 | tf_op jit(solution)/shard_map/reduce_scatter | solution.py:129
  89.6 60.5 %copy-start.7 = (s32[1,256]{1,0:T(1,128)S(1)}, s32[1,256]{1,0:T(1,128)}, u32[]{:S(2)}) copy-start(s32[1,256]{1,0:T(1,128)} %param.24) | copy-start | bytes 3076
  164.3 2.0 copy-start.1
  172.6 109.1 %copy-start.3 = (bf16[1,32,2048]{2,1,0:T(8,128)(2,1)S(1)}, bf16[1,32,2048]{2,1,0:T(8,128)(2,1)}, u32[]{:S(2)}) copy-start(bf16[1,32,2048]{2,1,0:T(8,128)(2,1)} %param.14) | copy-start | bytes 393220
  172.6 110.2 %copy-start.6 = (f32[2048]{0:T(1024)S(1)}, f32[2048]{0:T(1024)}, u32[]{:S(2)}) copy-start(f32[2048]{0:T(1024)} %param.19) | copy-start | bytes 24580
  172.6 113.4 %all-gather.12.cloned.1.call-start = ((), (), s32[]{:S(2)}) async-start(), calls=%async_computation.6 | async-start | bytes 1179648 | tf_op jit(solution)/shard_map/all_gather | solution.py:138
  173.2 168.9 %all-gather.10.cloned.1.call-start = ((), (), s32[]{:S(2)}) async-start(), calls=%async_computation.5 | async-start | bytes 4325376 | tf_op jit(solution)/shard_map/all_gather | solution.py:136
  284.4 96.3 %all-gather.14.cloned.1.call-start = ((), (), s32[]{:S(2)}) async-start(), calls=%async_computation.7 | async-start | bytes 1179648 | tf_op jit(solution)/shard_map/all_gather | solution.py:139
  285.0 138.1 %all-gather.16.cloned.1.call-start = ((), (), s32[]{:S(2)}) async-start(), calls=%async_computation.8 | async-start | bytes 1179648 | tf_op jit(solution)/shard_map/all_gather | solution.py:140
  285.8 247.6 %reduce-scatter.5.cloned.1.call-start = ((), (), s32[]{:S(2)}) async-start(), calls=%async_computation.9 | async-start | bytes 4325376 | tf_op jit(solution)/shard_map/reduce_scatter | solution.py:147
  432.3 101.1 %copy-start.4 = (bf16[32,2048]{1,0:T(8,128)(2,1)S(1)}, bf16[32,2048]{1,0:T(8,128)(2,1)}, u32[]{:S(2)}) copy-start(bf16[32,2048]{1,0:T(8,128)(2,1)} %reduce-scatter.3.cloned.1.call-done) | copy-start | bytes 393220
Sparse Core Ops, SparseCore 0:
  11.4 63.1 all-gather.17
  80.3 67.9 all-gather.7
  172.7 108.9 reduce-scatter.2
Sparse Core Ops, SparseCore 1:
  174.9 48.2 all-gather.11
  284.5 57.5 all-gather.9
  343.8 37.0 all-gather.13
  382.6 40.5 all-gather.15
  432.5 100.9 reduce-scatter.4
where the time goes:
time: 543 us; the launch traced here: 542 us
  waiting for transfers between devices  464 us (85%)
  matrix products  29.7 us (5%)
  between operations  16.5 us (3%)
  other arithmetic  16.4 us (3%)
  local copies, waits for them, and re-layouts  8.66 us (2%)
  starting transfers between devices  7.14 us (1%)
    reduce_scatter x1, waiting for transfers between devices, on_device(): lax.psum_scatter(jnp.dot(rows_in, out_weight, preferred_element_type=jnp....  108 us
    reduce_scatter x1, waiting for transfers between devices, on_device(): lax.psum_scatter(jnp.dot(activated, down_rows, preferred_element_type=jnp...  98.5 us
    all_gather x1, waiting for transfers between devices, on_device(): all_tokens = lax.all_gather(own_tokens, 'dev', axis=0, tiled=True)  65.8 us
    all_gather x1, waiting for transfers between devices, on_device(): lax.all_gather(root_norm(residual, feedforward_gain), 'dev', axis=0, tile...  56.1 us
    all_gather x1, waiting for transfers between devices, on_device(): keyval_all = lax.all_gather(raw_columns, 'dev', axis=0, tiled=True)  55 us
    all_gather x1, waiting for transfers between devices, on_device(): lax.all_gather(down_weight, 'req', axis=0, tiled=True)  42.4 us
    all_gather x1, waiting for transfers between devices, on_device(): lax.all_gather(up_weight, 'req', axis=0, tiled=True)  34.9 us
    dot_general x8, matrix products, transposed_product(): lax.dot_general(left, right, (((1,), (1,)), ((), ())), preferred_element_...  12.1 us
  transfers between devices with their start and end apart: 9, of which 7 were waited for; matrix products, arithmetic and copies ran while one was open for 3% of the time, Pallas kernels for 0%

commit v1 on v0

--- a/solution.py
+++ b/solution.py
@@ -75,7 +75,10 @@
     member = lax.axis_index("dev")
     length = prefix_length[0]
     own_tokens = hidden_in[0]
-    all_tokens = lax.all_gather(own_tokens, "dev", axis=0, tiled=True)
+    size = lax.axis_size("dev")
+    blocks = jnp.stack([own_tokens for _ in range(size)])
+    blocks = lax.all_to_all(blocks, "dev", split_axis=0, concat_axis=0)
+    all_tokens = jnp.concatenate(blocks, axis=0)
     normed = root_norm(all_tokens, attention_gain)
     positions = length + jnp.arange(all_count, dtype=jnp.int32)
     raw_columns = transposed_product(keyval_weight, normed).astype(jnp.bfloat16)

time: 543 us -> 582 us (1.072)
  blocking collectives: 0 us -> 107 us
  waiting for transfers between devices: 464 us -> 391 us
    all_to_all x0 -> x1, blocking collectives: none -> 107 us  [on_device(): blocks = lax.all_to_all(blocks, 'dev', split_axis=0, concat_axis=0)]
    all_gather x1 -> x0, waiting for transfers between devices: 65.8 us -> none  [on_device(): all_tokens = lax.all_gather(own_tokens, 'dev', axis=0, tiled=True)]
    all_gather x1, waiting for transfers between devices: 55 us -> 48.2 us  [on_device(): keyval_all = lax.all_gather(raw_columns, 'dev', axis=0, tiled=True)]
  transfers between devices with their start and end apart: 9 -> 8, of which waited for: 7 -> 6; matrix products, arithmetic and copies ran while one was open for 3% -> 3% of each run, Pallas kernels for 0% -> 0%
where the time goes in v1:
time: 582 us
  waiting for transfers between devices  391 us (67%)
  blocking collectives  107 us (18%)
  matrix products  29.5 us (5%)
  other arithmetic  17.4 us (3%)
  between operations  16.5 us (3%)
  local copies, waits for them, and re-layouts  13.9 us (2%)
    reduce_scatter x1, waiting for transfers between devices, on_device(): lax.psum_scatter(jnp.dot(rows_in, out_weight, preferred_element_type=jnp....  109 us
    all_to_all x1, blocking collectives, on_device(): blocks = lax.all_to_all(blocks, 'dev', split_axis=0, concat_axis=0)  107 us
    reduce_scatter x1, waiting for transfers between devices, on_device(): lax.psum_scatter(jnp.dot(activated, down_rows, preferred_element_type=jnp...  99 us
    all_gather x1, waiting for transfers between devices, on_device(): lax.all_gather(root_norm(residual, feedforward_gain), 'dev', axis=0, tile...  56 us
    all_gather x1, waiting for transfers between devices, on_device(): keyval_all = lax.all_gather(raw_columns, 'dev', axis=0, tiled=True)  48.2 us
    all_gather x1, waiting for transfers between devices, on_device(): lax.all_gather(down_weight, 'req', axis=0, tiled=True)  42.4 us
    all_gather x1, waiting for transfers between devices, on_device(): lax.all_gather(up_weight, 'req', axis=0, tiled=True)  34.9 us
    dot_general x8, matrix products, transposed_product(): lax.dot_general(left, right, (((1,), (1,)), ((), ())), preferred_element_...  12 us
  transfers between devices with their start and end apart: 8, of which 6 were waited for; matrix products, arithmetic and copies ran while one was open for 3% of the time, Pallas kernels for 0%

profile of v1, /device:TPU:8, one launch (start us, length us, event | category | flops | bytes accessed | tf_op | source)
XLA Modules:
  0.0 581.7 jit_solution(6139534310196829828)
XLA Ops:
  8.1 1.5 stack.3
  9.5 107.5 %all_to_all.20 = bf16[32,32,2048]{2,1,0:T(8,128)(2,1)S(1)} all-to-all(bf16[32,32,2048]{2,1,0:T(8,128)(2,1)S(1)} %stack.3), channel_id=1, replica_groups=mesh['req'=8,'dev'=32] {'dev'}, dimensions={0} | all-to-all | bytes 8388608 | tf_op jit(solution)/shard_map/all_to_all | solution.py:80
  117.0 1.9 copy-done.2
  118.9 0.9 multiply_reduce_fusion
  119.9 3.3 fusion.12
  123.2 2.0 copy-done.1
  125.2 2.0 fusion.23
  127.3 0.8 gather_fusion.1
  128.1 1.1 select_bitcast_fusion
  129.3 5.1 all-to-all-start
  135.1 3.6 convolution_bitcast_fusion
  138.8 48.2 %all-gather.6.cloned.1.call-done = bf16[1024,1024]{1,0:T(8,128)(2,1)} async-done(((bf16[32,1024]{1,0:T(8,128)(2,1)}), bf16[1024,1024]{1,0:T(8,128)(2,1)}) %all-gather.6.cloned.1.call-update) | async-done | bytes 2097168 | tf_op jit(solution)/shard_map/all_gather | solution.py:85
  187.0 1.0 dynamic-slice_bitcast_fusion
  188.9 13.4 %while.14 = (s32[]{:T(128)}, f32[1024]{0:T(1024)S(1)}, f32[1024]{0:T(1024)S(1)}, f32[1024,64]{0,1:T(8,128)S(1)}, s32[]{:T(128)}, /*index=5*/s32[]{:T(128)}, s32[...) while((s32[]{:T(128)}, f32[1024]{0:T(1024)S(1)}, ...), condition=%wide.region_4.5_spmd, body=%wide.region_1.4_spmd.sunk | while | flops 139661504 | bytes 7807755 | solution.py:126
  189.9 0.7 add_compare_fusion.2
  193.2 0.7 add_compare_fusion.2
  202.2 0.8 fusion.14
  203.0 2.0 copy-done.3
  205.5 5.8 convolution_convert_fusion.1
  211.9 108.7 %reduce-scatter.3.cloned.1.call-done = bf16[32,2048]{1,0:T(8,128)(2,1)} async-done(((bf16[1024,2048]{1,0:T(8,128)(2,1)}), bf16[32,2048]{1,0:T(8,128)(2,1)}) %reduce-scatter.3.cloned.1.call-update) | async-done | bytes 131088 | tf_op jit(solution)/shard_map/reduce_scatter | solution.py:132
  320.7 1.1 multiply_reduce_fusion.1
  321.7 1.7 multiply_convert_fusion
  324.0 0.7 all-gather.14.cloned.1.call-update
  325.0 56.0 %all-gather.8.cloned.1.call-done = bf16[1024,2048]{1,0:T(8,128)(2,1)} async-done(((bf16[32,2048]{1,0:T(8,128)(2,1)}), bf16[1024,2048]{1,0:T(8,128)(2,1)}) %all-gather.8.cloned.1.call-update) | async-done | bytes 4194320 | tf_op jit(solution)/shard_map/all_gather | solution.py:139
  381.0 3.8 fusion.74
  384.8 34.9 %all-gather.12.cloned.1.call-done = bf16[256,2048]{1,0:T(8,128)(2,1)} async-done(((bf16[32,2048]{1,0:T(8,128)(2,1)}), bf16[256,2048]{1,0:T(8,128)(2,1)}) %all-gather.12.cloned.1.call-update) | async-done | bytes 1048592 | tf_op jit(solution)/shard_map/all_gather | solution.py:142
  419.7 42.4 %all-gather.14.cloned.1.call-done = bf16[256,2048]{1,0:T(8,128)(2,1)} async-done(((bf16[32,2048]{1,0:T(8,128)(2,1)}), bf16[256,2048]{1,0:T(8,128)(2,1)}) %all-gather.14.cloned.1.call-update) | async-done | bytes 1048592 | tf_op jit(solution)/shard_map/all_gather | solution.py:143
  462.1 9.2 %convolution_convert_fusion = bf16[1024,2048]{1,0:T(8,128)(2,1)} fusion(bf16[256,2048]{1,0:T(8,128)(2,1)} %all-gather.14.cloned.1.call-done, bf16[1024,2048]{1,0:T(8,128)(2,1)} %all-gather.8.cloned.1.call-done, bf16[256,2048]{1,0:T(8,128)(2,1)} %all-gather.12.cloned.1.call-done, f32[1024,256]{1,0:T(8,128)S(1)} %fusion.74), kind=kOutput, calls=%fused_computation.29 | convolution fusion | flops 2151153664 | bytes 11534336 | tf_op jit(solution)/shard_map/dot_general | solution.py:151
  471.5 1.1 constant_dynamic-slice_fusion
  473.0 0.7 maximum_bitcast_fusion.2
  473.8 99.0 %reduce-scatter.5.cloned.1.call-done = bf16[32,2048]{1,0:T(8,128)(2,1)} async-done(((bf16[1024,2048]{1,0:T(8,128)(2,1)}), bf16[32,2048]{1,0:T(8,128)(2,1)}) %reduce-scatter.5.cloned.1.call-update) | async-done | bytes 131088 | tf_op jit(solution)/shard_map/reduce_scatter | solution.py:150
  572.8 1.6 fusion.56
  (113 shorter events, 15.4 us)
Async XLA Ops:
  8.0 197.5 %copy-start = (bf16[64,2048]{1,0:T(8,128)(2,1)S(1)}, bf16[64,2048]{1,0:T(8,128)(2,1)}, u32[]{:S(2)}) copy-start(bf16[64,2048]{1,0:T(8,128)(2,1)} %param.18) | copy-start | bytes 786436
  8.0 179.0 %all-gather.6.cloned.1.call-start = ((), (), s32[]{:S(2)}) async-start(), calls=%async_computation.4 | async-start | bytes 2162688 | tf_op jit(solution)/shard_map/all_gather | solution.py:85
  117.0 1.9 copy-start.2
  118.9 1.0 copy-start.9
  119.9 5.3 copy-start.8
  123.2 2.0 copy-start.1
  125.2 2.0 copy-start.7
  127.2 7.9 %copy-start.6 = (bf16[64,2048]{1,0:T(8,128)(2,1)S(1)}, bf16[64,2048]{1,0:T(8,128)(2,1)}, u32[]{:S(2)}) copy-start(bf16[64,2048]{1,0:T(8,128)(2,1)} %param.16) | copy-start | bytes 786436
  129.3 59.5 %all-to-all-start = ((bf16[8,16,32,128]{3,1,0,2:T(8,128)(2,1)}), bf16[8,16,32,128]{3,1,0,2:T(8,128)(2,1)S(1)}, u32[]{:S(2)}, u32[]{:S(2)}) async-start(bf16[8,16,32,128]{3,1,0,2:T(8,128)(2,1)} %select_bitcast_fusion), calls=%async_computation | async-start | bytes 2097152 | tf_op jit(solution)/shard_map/all_to_all | solution.py:107
  134.3 186.3 %reduce-scatter.3.cloned.1.call-start = ((), (), s32[]{:S(2)}) async-start(), calls=%async_computation.5 | async-start | bytes 4325376 | tf_op jit(solution)/shard_map/reduce_scatter | solution.py:132
  135.1 53.7 %copy-start.11 = (s32[1,256]{1,0:T(1,128)S(1)}, s32[1,256]{1,0:T(1,128)}, u32[]{:S(2)}) copy-start(s32[1,256]{1,0:T(1,128)} %param.24) | copy-start | bytes 3076
  203.0 2.0 copy-start.3
  211.3 109.4 %copy-start.4 = (bf16[1,32,2048]{2,1,0:T(8,128)(2,1)S(1)}, bf16[1,32,2048]{2,1,0:T(8,128)(2,1)}, u32[]{:S(2)}) copy-start(bf16[1,32,2048]{2,1,0:T(8,128)(2,1)} %param.14) | copy-start | bytes 393220
  211.3 110.5 %copy-start.10 = (f32[2048]{0:T(1024)S(1)}, f32[2048]{0:T(1024)}, u32[]{:S(2)}) copy-start(f32[2048]{0:T(1024)} %param.19) | copy-start | bytes 24580
  211.3 113.7 %all-gather.10.cloned.1.call-start = ((), (), s32[]{:S(2)}) async-start(), calls=%async_computation.7 | async-start | bytes 1179648 | tf_op jit(solution)/shard_map/all_gather | solution.py:141
  211.9 169.1 %all-gather.8.cloned.1.call-start = ((), (), s32[]{:S(2)}) async-start(), calls=%async_computation.6 | async-start | bytes 4325376 | tf_op jit(solution)/shard_map/all_gather | solution.py:139
  323.4 96.3 %all-gather.12.cloned.1.call-start = ((), (), s32[]{:S(2)}) async-start(), calls=%async_computation.8 | async-start | bytes 1179648 | tf_op jit(solution)/shard_map/all_gather | solution.py:142
  324.0 138.1 %all-gather.14.cloned.1.call-start = ((), (), s32[]{:S(2)}) async-start(), calls=%async_computation.9 | async-start | bytes 1179648 | tf_op jit(solution)/shard_map/all_gather | solution.py:143
  324.7 248.0 %reduce-scatter.5.cloned.1.call-start = ((), (), s32[]{:S(2)}) async-start(), calls=%async_computation.10 | async-start | bytes 4325376 | tf_op jit(solution)/shard_map/reduce_scatter | solution.py:150
  471.3 101.5 %copy-start.5 = (bf16[32,2048]{1,0:T(8,128)(2,1)S(1)}, bf16[32,2048]{1,0:T(8,128)(2,1)}, u32[]{:S(2)}) copy-start(bf16[32,2048]{1,0:T(8,128)(2,1)} %reduce-scatter.3.cloned.1.call-done) | copy-start | bytes 393220
Sparse Core Ops, SparseCore 0:
  127.3 59.6 all-gather.5
  211.4 109.1 reduce-scatter.2
  471.4 101.2 reduce-scatter.4
Sparse Core Ops, SparseCore 1:
  213.6 48.3 all-gather.9
  323.5 57.5 all-gather.7
  382.7 37.0 all-gather.11
  421.5 40.5 all-gather.13
